TPU v7x, 256 devices: a whole 4x4x8 slice. The times are simulated.
256 devices in a mesh: section: 2 (over core), dp: 8 (over y, z_lo), tensor: 16 (over x, z_hi).
Axes of the slice: x: 4, y: 4, z: 8 (z_hi: 4, z_lo: 2; z = z_hi * 2 + z_lo), core: 2. Of those that a mesh axis runs over, the one named last changes fastest.
Arguments:
- residual_parts: bfloat16 [2, 3072, 16384], P('section', 'dp', 'tensor'), may hold values from -120 to 120
- attn_out: bfloat16 [2, 3072, 16384], P('section', 'dp', 'tensor'), may hold values from -6 to 6
- ffn_input: bfloat16 [2, 3072, 53248], P('section', 'dp', 'tensor'), may hold values from -6 to 6
- norm_gain: float32 [2, 16384], P('section', 'tensor'), may hold values from 0.25 to 1.75
- mixing: bfloat16 [2, 52, 52], P('section'), may hold values from -0.875 to 0.875
- blocks: int32 [2, 2], P('section'), may hold values from 0 to 25, as said below
Outputs:
- hess_in: float32 [2, 16384, 1024], P('section', 'tensor', 'dp')
- hess_o: float32 [2, 16384, 1024], P('section', 'tensor', 'dp')
- hess_down: float32 [2, 2048, 2048], P('section', 'tensor', 'dp')
Inputs may be any that keep to these rules, and one draw needn't show every extreme that they name: `blocks`: entry [s, 0] is below 16; entry [s, 1] is below 26. In every draw one layer has entry [s, 0] = 0 and entry [s, 1] = 25.
All inputs are finite; a program needn't handle non-finite values.
Results may differ from a plain program's by a relative error of at most 0.0038.
Values may be sent and summed in bfloat16 or wider, within the bound.
No kernel may reach another device: no remote copies, remote signals or barrier semaphores. Data moves between devices by JAX's collectives and lax.ppermute only.
A program may use at most 64 MiB of HBM per device.

v0:
```python
import math
import jax
import jax.numpy as jnp
from jax import lax
from jax.sharding import Mesh
from jax.sharding import PartitionSpec as P

D = 16384
KB = 52
HBLK = 1024
BLK = 2048
TENSOR = ("tensor_0", "tensor_1")
EPS = 1e-05


def passed_along(x, axis, by):
    devices = lax.axis_size(axis)
    pairs = [(i, i + by) for i in range(devices) if 0 <= i + by < devices]
    return lax.ppermute(x, axis, pairs)


def copy_for_each(x, axis):
    devices = lax.axis_size(axis)
    return lax.all_to_all(jnp.broadcast_to(x[None], (devices, *x.shape)), axis, 0, 0, tiled=True)


def over_copies(x, axis):
    everything = copy_for_each(x, axis)
    return jnp.sum(everything, axis=0)


def broadcast_by_axis(x, axes, root):
    x = jnp.where(lax.axis_index(axes) == root, x, jnp.zeros_like(x))
    for axis in axes:
        x = lax.psum(x, axis)
    return x


def in_blocks(x, dim, devices):
    before, after = (x.shape[:dim], x.shape[dim + 1 :])
    return jnp.moveaxis(x.reshape(*before, devices, -1, *after), dim, 0)


def summed_on_arrival(x, axis, dim):
    tiles = in_blocks(x, dim, lax.axis_size(axis))
    arrived = lax.all_to_all(tiles, axis, split_axis=0, concat_axis=0, tiled=True)
    return arrived.sum(axis=0)


def in_one_piece(arrays, axis, dim, along):
    both = jnp.concatenate(arrays, axis=along)
    out, at, done = (lax.psum_scatter(both, axis, scatter_dimension=dim, tiled=True), 0, [])
    for a in arrays:
        done.append(lax.slice_in_dim(out, at, at + a.shape[along], axis=along))
        at += a.shape[along]
    return tuple(done)


def bit_parity(values):
    total = jnp.zeros_like(values)
    for position in range(16):
        total = total + values // (1 << position) % 2
    return total % 2


def sylvester(order):
    index = jnp.arange(order, dtype=jnp.int32)
    parity = bit_parity(jnp.bitwise_and(index[:, None], index[None, :]))
    return (1 - 2 * parity).astype(jnp.float32)


def gram(left, right):
    return lax.dot_general(
        left, right, (((0,), (0,)), ((), ())), preferred_element_type=jnp.float32
    )


def local(residual_parts, attn_out, ffn_input, norm_gain, mixing, blocks):
    local_d = residual_parts.shape[2]
    local_f = ffn_input.shape[2]
    token_rows = residual_parts.shape[1]
    own_part = residual_parts[0]
    earlier = passed_along(own_part, "section", 1)
    layer_in = earlier.astype(jnp.float32) + own_part.astype(jnp.float32)
    square_total = over_copies(jnp.sum(layer_in * layer_in, axis=1), TENSOR)
    normed = (layer_in * lax.rsqrt(square_total / D + EPS)[:, None] * norm_gain[0][None, :]).astype(
        jnp.bfloat16
    )
    attention = attn_out[0]
    first_col = blocks[0, 0] * HBLK
    norm_list, attn_list = ([], [])
    owner = first_col // local_d + 0
    norm_got = broadcast_by_axis(normed, TENSOR, owner)
    attn_got = broadcast_by_axis(attention, TENSOR, owner)
    norm_list.append(norm_got)
    attn_list.append(attn_got)
    norm_block = norm_list[0]
    attn_block = attn_list[0]
    tensor_count = lax.axis_size(TENSOR)
    member = lax.axis_index(TENSOR)
    a_local = local_f // KB
    order_a = a_local * tensor_count
    cube = ffn_input[0].reshape(token_rows, a_local, KB)
    mixed = jnp.einsum("rak,kc->rac", cube, mixing[0], preferred_element_type=jnp.float32)
    turned = jnp.einsum("rac,ae->rec", mixed, sylvester(a_local), precision=lax.Precision.HIGHEST)
    turned = turned.reshape(token_rows, local_f)
    start = blocks[0, 1] * BLK
    doubled = jnp.concatenate([turned, turned], axis=1)
    window = lax.dynamic_slice_in_dim(doubled, start % local_f, BLK, 1)
    target = (start + jnp.arange(BLK, dtype=jnp.int32)) // local_f
    parity = bit_parity(jnp.bitwise_and(target, member))
    signs = (1 - 2 * parity).astype(jnp.float32) / math.sqrt(order_a)
    term = window * signs[None, :]
    own_cols = summed_on_arrival(term, TENSOR, 1).astype(jnp.bfloat16)
    rotated = lax.all_gather(own_cols, TENSOR, axis=1, tiled=True)
    part_in = gram(normed, norm_block)
    part_o = gram(attention, attn_block)
    part_down = gram(own_cols, rotated)
    summed = (
        *in_one_piece((part_in, part_o), "dp", 1, 0),
        lax.psum_scatter(part_down, "dp", scatter_dimension=1, tiled=True),
    )
    scale = 2.0 / (token_rows * lax.axis_size("dp"))
    hess_in = (scale * summed[0])[None]
    hess_o = (scale * summed[1])[None]
    hess_down = (scale * summed[2])[None]
    return (hess_in, hess_o, hess_down)


def solution(mesh):
    finer = Mesh(
        mesh.devices.reshape(mesh.shape["section"], mesh.shape["dp"], 4, 4),
        ("section", "dp", "tensor_0", "tensor_1"),
    )
    in_specs = (
        P("section", "dp", TENSOR),
        P("section", "dp", TENSOR),
        P("section", "dp", TENSOR),
        P("section", TENSOR),
        P("section", None, None),
        P("section", None),
    )
    out_specs = (P("section", TENSOR, "dp"), P("section", TENSOR, "dp"), P("section", TENSOR, "dp"))
    return jax.shard_map(local, mesh=finer, in_specs=in_specs, out_specs=out_specs, check_vma=False)
```

profile of v0, /device:TPU:1, one launch (start us, length us, event | category | flops | bytes accessed | tf_op | source)
XLA Modules:
  0.0 455.9 jit_solution(6343559055614895578)
XLA Ops:
  8.0 0.0 copy-start
  8.0 1.3 collective-permute-start
  9.3 4.4 copy.20
  13.7 3.4 reshape_squeeze.3
  17.1 0.0 copy-done
  17.1 0.0 copy-start.9
  17.1 3.3 fusion.156
  20.4 0.0 copy-done.9
  20.4 0.6 fusion.253
  21.7 8.3 %fusion.4 = f32[384,64,52]{0,1,2:T(8,128)S(1)} fusion(f32[384,64,52]{0,2,1:T(8,128)} %fusion.156), kind=kOutput, calls=%fused_computation.7 | convolution fusion | flops 982917120 | bytes 10223616 | tf_op jit(solution)/shard_map/rac,ae->rec/dot_general | solution.py:105
  30.0 5.4 %copy.23 = f32[384,64,52]{0,2,1:T(8,128)} copy(f32[384,64,52]{0,1,2:T(8,128)S(1)} %fusion.4) | data formatting | bytes 10223616 | tf_op jit(solution)/shard_map/rac,ae->rec/transpose | solution.py:105
  35.4 0.0 copy-start.1
  35.4 6.4 %reshape.401 = f32[384,3328]{0,1:T(8,128)} reshape(f32[384,64,52]{0,2,1:T(8,128)} %copy.23) | data formatting | bytes 10223616 | tf_op jit(solution)/shard_map/reshape | solution.py:106
  41.7 0.1 fusion.207
  41.9 0.0 collective-permute-done
  41.9 0.0 copy-done.1
  41.9 0.0 copy-start.3
  41.9 0.3 multiply_reduce_fusion
  42.2 0.6 broadcast_in_dim.8
  42.8 11.6 %all-to-all-start = ((f32[16,1,384]{2,1,0:T(1,128)}), f32[16,1,384]{2,1,0:T(1,128)S(1)}, u32[]{:S(2)}, u32[]{:S(2)}) async-start(f32[16,1,384]{2,1,0:T(1,128)} %broadcast_in_dim.8), calls=%async_computation | async-start | bytes 49152 | tf_op jit(solution)/shard_map/all_to_all | solution.py:24
  54.5 4.5 fusion.3
  59.0 0.0 copy-done.3
  59.0 4.3 all-to-all-done
  63.3 0.0 copy-start.8
  63.3 0.0 copy-start.7
  63.3 0.6 copy-done.8
  63.9 4.7 %all-to-all-start.1 = ((f32[16,384,128]{1,2,0:T(8,128)}), f32[16,384,128]{1,2,0:T(8,128)S(1)}, u32[]{:S(2)}, u32[]{:S(2)}) async-start(f32[16,384,128]{1,2,0:T(8,128)} %bitcast.13), calls=%async_computation.2 | async-start | bytes 6291456 | tf_op jit(solution)/shard_map/all_to_all | solution.py:46
  68.6 0.0 all-reduce.7.cloned.1.call-start
  69.3 2.1 bitcast_select_fusion
  71.4 0.8 reduce_sum.28
  72.2 0.0 copy-done.7
  72.2 2.6 broadcast_select_fusion
  74.8 0.0 all-reduce.7.cloned.1.call-update
  74.9 0.0 all-gather.2.cloned.1.call-start
  74.9 62.6 %all-to-all-done.1 = f32[16,384,128]{1,2,0:T(8,128)S(1)} async-done(((f32[16,384,128]{1,2,0:T(8,128)}), f32[16,384,128]{1,2,0:T(8,128)S(1)}, u32[]{:S(2)}, u32[]{:S(2)}) %all-to-all-start.1) | async-done | bytes 3145760 | tf_op jit(solution)/shard_map/all_to_all | solution.py:46
  137.5 0.8 reduce_sum.29
  138.3 0.0 copy-start.5
  138.3 0.0 all-gather.2.cloned.1.call-update
  138.4 0.0 all-reduce.5.cloned.1.call-start
  138.4 15.9 %all-reduce.7.cloned.1.call-done = (bf16[384,1024]{1,0:T(8,128)(2,1)}, bf16[384,1024]{1,0:T(8,128)(2,1)}) async-done(((bf16[384,1024]{1,0:T(8,128)(2,1)}, bf16[384,1024]{1,0:T(8,128)(2,1)}), (bf16[384,1024]{1,0:T(8,128)(2,1)}, bf16[384,1024]{1,0:T(8,128)(2,1)})) %all-reduce.7.cloned.1.call-update) | async-done | bytes 1572880 | tf_op jit(solution)/shard_map/psum | solution.py:35
  154.3 0.0 all-reduce.5.cloned.1.call-update
  154.4 0.0 reduce-scatter.5.cloned.1.call-start
  154.4 56.3 %all-gather.2.cloned.1.call-done = bf16[384,2048]{0,1:T(8,128)(2,1)} async-done(((bf16[384,128]{0,1:T(8,128)(2,1)}), bf16[384,2048]{0,1:T(8,128)(2,1)}) %all-gather.2.cloned.1.call-update) | async-done | bytes 1572880 | tf_op jit(solution)/shard_map/all_gather | solution.py:115
  210.7 3.1 fusion.254
  213.8 0.0 reduce-scatter.5.cloned.1.call-update
  213.8 0.0 reduce-scatter.3.cloned.1.call-start
  213.9 41.1 %all-reduce.5.cloned.1.call-done = (bf16[384,1024]{1,0:T(8,128)(2,1)}, bf16[384,1024]{1,0:T(8,128)(2,1)}) async-done(((bf16[384,1024]{1,0:T(8,128)(2,1)}, bf16[384,1024]{1,0:T(8,128)(2,1)}), (bf16[384,1024]{1,0:T(8,128)(2,1)}, bf16[384,1024]{1,0:T(8,128)(2,1)})) %all-reduce.5.cloned.1.call-update) | async-done | bytes 1572880 | tf_op jit(solution)/shard_map/psum | solution.py:35
  255.0 0.0 copy-done.5
  255.0 0.0 copy-start.2
  255.0 0.0 copy-start.4
  255.0 0.0 copy-start.6
  255.0 2.6 convolution_bitcast_fusion
  257.6 0.0 copy-done.2
  257.6 0.0 copy-done.4
  257.7 0.0 copy-done.6
  257.7 1.4 fusion.252
  259.1 4.1 pad_maximum_fusion
  263.2 0.0 reduce-scatter.3.cloned.1.call-update
  263.2 6.4 %reduce-scatter.5.cloned.1.call-done = f32[128,256]{1,0:T(8,128)} async-done(((f32[128,2048]{1,0:T(8,128)}), f32[128,256]{1,0:T(8,128)}) %reduce-scatter.5.cloned.1.call-update) | async-done | bytes 131088 | tf_op jit(solution)/shard_map/reduce_scatter | solution.py:121
  269.6 1.6 multiply_bitcast_fusion
  271.1 174.9 %reduce-scatter.3.cloned.1.call-done = f32[2048,128]{1,0:T(8,128)} async-done(((f32[2048,1024]{1,0:T(8,128)}), f32[2048,128]{1,0:T(8,128)}) %reduce-scatter.3.cloned.1.call-update) | async-done | bytes 1048592 | tf_op jit(solution)/shard_map/reduce_scatter | solution.py:52
  446.1 2.3 fusion.8
  (1 shorter events, 0.0 us)
Async XLA Ops:
  8.0 9.1 %copy-start = (bf16[1,52,52]{2,1,0:T(8,128)(2,1)S(1)}, bf16[1,52,52]{2,1,0:T(8,128)(2,1)}, u32[]{:S(2)}) copy-start(bf16[1,52,52]{2,1,0:T(8,128)(2,1)} %param.10) | copy-start | bytes 16228
  8.0 33.8 %collective-permute-start = (bf16[384,1024]{1,0:T(8,128)(2,1)}, bf16[384,1024]{1,0:T(8,128)(2,1)S(1)}, u32[]{:S(2)}, u32[]{:S(2)}) collective-permute-start(bf16[384,1024]{1,0:T(8,128)(2,1)} %bitcast.43), channel_id=1, source_target_pairs={{0,128},{1,129},{2,130},{3,131},{4,132},{5,133},{6,134},{7,135},{8... | collective-permute-start | bytes 2359304 | tf_op jit(solution)/shard_map/ppermute | solution.py:19
  17.1 3.3 copy-start.9
  35.4 6.5 %copy-start.1 = (bf16[1,384,1024]{2,1,0:T(8,128)(2,1)S(1)}, bf16[1,384,1024]{2,1,0:T(8,128)(2,1)}, u32[]{:S(2)}) copy-start(bf16[1,384,1024]{2,1,0:T(8,128)(2,1)} %param.6) | copy-start | bytes 2359300
  41.9 17.1 %copy-start.3 = (bf16[384,1024]{1,0:T(8,128)(2,1)}, bf16[384,1024]{1,0:T(8,128)(2,1)S(1)}, u32[]{:S(2)}) copy-start(bf16[384,1024]{1,0:T(8,128)(2,1)S(1)} %collective-permute-done) | copy-start | bytes 2359300
  42.8 20.4 %all-to-all-start = ((f32[16,1,384]{2,1,0:T(1,128)}), f32[16,1,384]{2,1,0:T(1,128)S(1)}, u32[]{:S(2)}, u32[]{:S(2)}) async-start(f32[16,1,384]{2,1,0:T(1,128)} %broadcast_in_dim.8), calls=%async_computation | async-start | bytes 49152 | tf_op jit(solution)/shard_map/all_to_all | solution.py:24
  63.3 0.6 copy-start.8
  63.3 8.9 %copy-start.7 = (f32[1,1024]{1,0:T(1,128)S(1)}, f32[1,1024]{1,0:T(1,128)}, u32[]{:S(2)}) copy-start(f32[1,1024]{1,0:T(1,128)} %param.9) | copy-start | bytes 12292
  63.9 73.6 %all-to-all-start.1 = ((f32[16,384,128]{1,2,0:T(8,128)}), f32[16,384,128]{1,2,0:T(8,128)S(1)}, u32[]{:S(2)}, u32[]{:S(2)}) async-start(f32[16,384,128]{1,2,0:T(8,128)} %bitcast.13), calls=%async_computation.2 | async-start | bytes 6291456 | tf_op jit(solution)/shard_map/all_to_all | solution.py:46
  68.6 85.7 %all-reduce.7.cloned.1.call-start = ((), (), s32[]{:S(2)}) async-start(), calls=%async_computation.8 | async-start | bytes 3145728 | tf_op jit(solution)/shard_map/psum | solution.py:35
  74.9 135.8 %all-gather.2.cloned.1.call-start = ((), (), s32[]{:S(2)}) async-start(), calls=%async_computation.5 | async-start | bytes 1671168 | tf_op jit(solution)/shard_map/all_gather | solution.py:115
  138.3 116.7 %copy-start.5 = (bf16[1,384,1024]{2,1,0:T(8,128)(2,1)S(1)}, bf16[1,384,1024]{2,1,0:T(8,128)(2,1)}, u32[]{:S(2)}) copy-start(bf16[1,384,1024]{2,1,0:T(8,128)(2,1)} %param.7) | copy-start | bytes 2359300
  138.4 116.7 %all-reduce.5.cloned.1.call-start = ((), (), s32[]{:S(2)}) async-start(), calls=%async_computation.7 | async-start | bytes 3145728 | tf_op jit(solution)/shard_map/psum | solution.py:35
  154.4 115.2 %reduce-scatter.5.cloned.1.call-start = ((), (), s32[]{:S(2)}) async-start(), calls=%async_computation.6 | async-start | bytes 1179648 | tf_op jit(solution)/shard_map/reduce_scatter | solution.py:121
  213.8 232.2 %reduce-scatter.3.cloned.1.call-start = ((), (), s32[]{:S(2)}) async-start(), calls=%async_computation.4 | async-start | bytes 9437184 | tf_op jit(solution)/shard_map/reduce_scatter | solution.py:52
  255.0 2.6 copy-start.2
  255.0 2.6 copy-start.4
  255.0 2.6 copy-start.6
Sparse Core Ops, SparseCore 0:
  75.0 79.3 all-reduce.6
  157.0 97.9 all-reduce.4
Sparse Core Ops, SparseCore 1:
  138.4 72.2 all-gather.1
  213.9 55.6 reduce-scatter.4
  272.0 174.0 reduce-scatter.2
where the time goes:
time: 457 us; the launch traced here: 456 us
  waiting for transfers between devices  362 us (79%)
  local copies, waits for them, and re-layouts  21.4 us (5%)
  other arithmetic  19.1 us (4%)
  matrix products  18.8 us (4%)
  starting transfers between devices  17.8 us (4%)
  between operations  17.2 us (4%)
    reduce_scatter x1, waiting for transfers between devices, in_one_piece(): lax.psum_scatter(both, axis, scatter_dimension=dim, tiled=True)  175 us
    all_to_all x1, waiting for transfers between devices, summed_on_arrival(): lax.all_to_all(tiles, axis, split_axis=0, concat_axis=0, tiled=True)  62.6 us
    psum x2, waiting for transfers between devices, broadcast_by_axis(): x = lax.psum(x, axis)  57.1 us
    all_gather x1, waiting for transfers between devices, local(): rotated = lax.all_gather(own_cols, TENSOR, axis=1, tiled=True)  56.3 us
    all_to_all x1, starting transfers between devices, copy_for_each(): lax.all_to_all(jnp.broadcast_to(x[None], (devices, *x.shape)), axis, 0, 0...  11.6 us
  transfers between devices with their start and end apart: 8, of which 7 were waited for; matrix products, arithmetic and copies ran while one was open for 12% of the time, Pallas kernels for 0%

commit v1 on v0

--- a/solution.py
+++ b/solution.py
@@ -32,7 +32,7 @@
 def broadcast_by_axis(x, axes, root):
     x = jnp.where(lax.axis_index(axes) == root, x, jnp.zeros_like(x))
     for axis in axes:
-        x = lax.psum(x, axis)
+        x = jnp.sum(lax.all_gather(x, axis), axis=0)
     return x
 
 

time: 457 us -> 567 us (1.24)
  waiting for transfers between devices: 362 us -> 459 us
  other arithmetic: 19.1 us -> 31.7 us
    all_gather x0 -> x4, waiting for transfers between devices: none -> 124 us  [broadcast_by_axis(): x = jnp.sum(lax.all_gather(x, axis), axis=0)]
    psum x2 -> x0, waiting for transfers between devices: 57.1 us -> none  [broadcast_by_axis(): x = lax.psum(x, axis)]
    reduce_scatter x1, waiting for transfers between devices: 6.36 us -> 36.9 us  [local(): lax.psum_scatter(part_down, 'dp', scatter_dimension=1, tiled=True)]
    reduce_sum x0 -> x4, other arithmetic: none -> 12.4 us  [broadcast_by_axis(): x = jnp.sum(lax.all_gather(x, axis), axis=0)]
  transfers between devices with their start and end apart: 8 -> 10, of which waited for: 7 -> 7; matrix products, arithmetic and copies ran while one was open for 12% -> 12% of each run, Pallas kernels for 0% -> 0%
where the time goes in v1:
time: 567 us; the launch traced here: 566 us
  waiting for transfers between devices  459 us (81%)
  other arithmetic  31.7 us (6%)
  local copies, waits for them, and re-layouts  23 us (4%)
  matrix products  19.6 us (3%)
  starting transfers between devices  17 us (3%)
  between operations  15.7 us (3%)
    reduce_scatter x1, waiting for transfers between devices, in_one_piece(): lax.psum_scatter(both, axis, scatter_dimension=dim, tiled=True)  176 us
    all_gather x4, waiting for transfers between devices, broadcast_by_axis(): x = jnp.sum(lax.all_gather(x, axis), axis=0)  124 us
    all_to_all x1, waiting for transfers between devices, summed_on_arrival(): lax.all_to_all(tiles, axis, split_axis=0, concat_axis=0, tiled=True)  61.8 us
    all_gather x1, waiting for transfers between devices, local(): rotated = lax.all_gather(own_cols, TENSOR, axis=1, tiled=True)  56.1 us
    reduce_scatter x1, waiting for transfers between devices, local(): lax.psum_scatter(part_down, 'dp', scatter_dimension=1, tiled=True)  36.9 us
    reduce_sum x4, other arithmetic, broadcast_by_axis(): x = jnp.sum(lax.all_gather(x, axis), axis=0)  12.4 us
  transfers between devices with their start and end apart: 10, of which 7 were waited for; matrix products, arithmetic and copies ran while one was open for 12% of the time, Pallas kernels for 0%

profile of v1, /device:TPU:1, one launch (start us, length us, event | category | flops | bytes accessed | tf_op | source)
XLA Modules:
  0.0 566.0 jit_solution(6381758772579402188)
XLA Ops:
  7.2 0.0 copy-start
  7.2 0.0 all-gather.9.cloned.1.call-start
  7.2 1.3 fusion.253
  9.2 2.1 broadcast_select_fusion
  11.3 0.0 all-gather.9.cloned.1.call-update
  11.3 1.3 collective-permute-start
  12.6 4.4 copy.20
  17.0 3.4 reshape_squeeze.3
  20.4 0.0 copy-done
  20.5 3.3 fusion.156
  24.5 8.4 %fusion.4 = f32[384,64,52]{0,1,2:T(8,128)S(1)} fusion(f32[384,64,52]{0,2,1:T(8,128)} %fusion.156), kind=kOutput, calls=%fused_computation.7 | convolution fusion | flops 982917120 | bytes 10223616 | tf_op jit(solution)/shard_map/rac,ae->rec/dot_general | solution.py:105
  32.9 5.4 copy.23
  38.3 6.4 %reshape.401 = f32[384,3328]{0,1:T(8,128)} reshape(f32[384,64,52]{0,2,1:T(8,128)} %copy.23) | data formatting | bytes 10223616 | tf_op jit(solution)/shard_map/reshape | solution.py:106
  44.7 0.1 fusion.207
  44.8 0.0 collective-permute-done
  44.8 0.0 copy-done.3
  44.8 0.0 copy-start.5
  44.8 0.3 multiply_reduce_fusion
  45.2 0.6 broadcast_in_dim.8
  45.8 10.7 %all-to-all-start = ((f32[16,1,384]{2,1,0:T(1,128)}), f32[16,1,384]{2,1,0:T(1,128)S(1)}, u32[]{:S(2)}, u32[]{:S(2)}) async-start(f32[16,1,384]{2,1,0:T(1,128)} %broadcast_in_dim.8), calls=%async_computation | async-start | bytes 49152 | tf_op jit(solution)/shard_map/all_to_all | solution.py:24
  56.5 4.5 fusion.3
  61.0 0.0 copy-done.5
  61.0 4.3 all-to-all-done
  65.4 0.6 copy-done.10
  66.0 4.7 all-to-all-start.1
  70.7 0.0 all-gather.13.cloned.1.call-start
  70.8 0.8 reduce_sum.76
  71.6 0.0 copy-done.9
  71.6 2.7 broadcast_select_fusion.1
  74.2 0.0 all-gather.13.cloned.1.call-update
  74.2 0.0 all-gather.11.cloned.1.call-start
  74.3 61.8 %all-to-all-done.1 = f32[16,384,128]{1,2,0:T(8,128)S(1)} async-done(((f32[16,384,128]{1,2,0:T(8,128)}), f32[16,384,128]{1,2,0:T(8,128)S(1)}, u32[]{:S(2)}, u32[]{:S(2)}) %all-to-all-start.1) | async-done | bytes 3145760 | tf_op jit(solution)/shard_map/all_to_all | solution.py:46
  136.1 0.8 reduce_sum.81
  136.9 0.0 all-gather.11.cloned.1.call-update
  136.9 0.0 all-gather.17.cloned.1.call-start
  137.0 0.0 all-gather.9.cloned.1.call-done
  137.0 3.6 reduce_sum.79
  140.6 0.0 all-gather.17.cloned.1.call-update
  140.7 0.0 all-gather.15.cloned.1.call-start
  140.7 0.0 all-gather.13.cloned.1.call-done
  140.7 3.6 reduce_sum.77
  144.4 0.0 all-gather.15.cloned.1.call-update
  144.4 0.0 reduce-scatter.5.cloned.1.call-start
  144.4 56.1 %all-gather.11.cloned.1.call-done = bf16[384,2048]{0,1:T(8,128)(2,1)} async-done(((bf16[384,128]{0,1:T(8,128)(2,1)}), bf16[384,2048]{0,1:T(8,128)(2,1)}) %all-gather.11.cloned.1.call-update) | async-done | bytes 1572880 | tf_op jit(solution)/shard_map/all_gather | solution.py:115
  200.6 0.0 copy-done.8
  200.6 3.0 fusion.254
  203.6 0.0 reduce-scatter.5.cloned.1.call-update
  203.6 0.0 reduce-scatter.3.cloned.1.call-start
  203.7 60.8 %all-gather.17.cloned.1.call-done = bf16[1536,1024]{1,0:T(8,128)(2,1)} async-done(((bf16[384,1024]{1,0:T(8,128)(2,1)}), bf16[1536,1024]{1,0:T(8,128)(2,1)}) %all-gather.17.cloned.1.call-update) | async-done | bytes 3145744 | tf_op jit(solution)/shard_map/all_gather | solution.py:35
  264.5 2.6 reduce_sum.80
  267.1 0.0 copy-done.7
  267.1 3.4 convolution_bitcast_fusion
  270.5 63.0 %all-gather.15.cloned.1.call-done = bf16[1536,1024]{1,0:T(8,128)(2,1)} async-done(((bf16[384,1024]{1,0:T(8,128)(2,1)}), bf16[1536,1024]{1,0:T(8,128)(2,1)}) %all-gather.15.cloned.1.call-update) | async-done | bytes 3145744 | tf_op jit(solution)/shard_map/all_gather | solution.py:35
  333.5 2.6 reduce_sum.78
  336.1 1.4 fusion.252
  337.5 0.8 copy-done.2
  338.3 4.2 pad_maximum_fusion
  342.5 0.0 reduce-scatter.3.cloned.1.call-update
  342.5 0.0 copy-start.1
  342.5 36.9 %reduce-scatter.5.cloned.1.call-done = f32[128,256]{1,0:T(8,128)} async-done(((f32[128,2048]{1,0:T(8,128)}), f32[128,256]{1,0:T(8,128)}) %reduce-scatter.5.cloned.1.call-update) | async-done | bytes 131088 | tf_op jit(solution)/shard_map/reduce_scatter | solution.py:121
  379.4 1.6 multiply_bitcast_fusion
  381.0 175.8 %reduce-scatter.3.cloned.1.call-done = f32[2048,128]{1,0:T(8,128)} async-done(((f32[2048,1024]{1,0:T(8,128)}), f32[2048,128]{1,0:T(8,128)}) %reduce-scatter.3.cloned.1.call-update) | async-done | bytes 1048592 | tf_op jit(solution)/shard_map/reduce_scatter | solution.py:52
  556.9 2.3 fusion.8
  559.1 0.0 copy-done.1
  (11 shorter events, 0.0 us)
Async XLA Ops:
  7.2 13.3 %copy-start = (bf16[1,52,52]{2,1,0:T(8,128)(2,1)S(1)}, bf16[1,52,52]{2,1,0:T(8,128)(2,1)}, u32[]{:S(2)}) copy-start(bf16[1,52,52]{2,1,0:T(8,128)(2,1)} %param.10) | copy-start | bytes 16228
  7.2 129.8 %all-gather.9.cloned.1.call-start = ((), (), s32[]{:S(2)}) async-start(), calls=%async_computation.4 | async-start | bytes 3932160 | tf_op jit(solution)/shard_map/all_gather | solution.py:35
  11.3 33.5 %collective-permute-start = (bf16[384,1024]{1,0:T(8,128)(2,1)}, bf16[384,1024]{1,0:T(8,128)(2,1)S(1)}, u32[]{:S(2)}, u32[]{:S(2)}) collective-permute-start(bf16[384,1024]{1,0:T(8,128)(2,1)} %bitcast.45), channel_id=1, source_target_pairs={{0,128},{1,129},{2,130},{3,131},{4,132},{5,133},{6,134},{7,135},{8... | collective-permute-start | bytes 2359304 | tf_op jit(solution)/shard_map/ppermute | solution.py:19
  38.3 6.5 %copy-start.3 = (bf16[1,384,1024]{2,1,0:T(8,128)(2,1)S(1)}, bf16[1,384,1024]{2,1,0:T(8,128)(2,1)}, u32[]{:S(2)}) copy-start(bf16[1,384,1024]{2,1,0:T(8,128)(2,1)} %param.6) | copy-start | bytes 2359300
  44.8 16.2 %copy-start.5 = (bf16[384,1024]{1,0:T(8,128)(2,1)}, bf16[384,1024]{1,0:T(8,128)(2,1)S(1)}, u32[]{:S(2)}) copy-start(bf16[384,1024]{1,0:T(8,128)(2,1)S(1)} %collective-permute-done) | copy-start | bytes 2359300
  45.8 19.6 %all-to-all-start = ((f32[16,1,384]{2,1,0:T(1,128)}), f32[16,1,384]{2,1,0:T(1,128)S(1)}, u32[]{:S(2)}, u32[]{:S(2)}) async-start(f32[16,1,384]{2,1,0:T(1,128)} %broadcast_in_dim.8), calls=%async_computation | async-start | bytes 49152 | tf_op jit(solution)/shard_map/all_to_all | solution.py:24
  65.4 0.6 copy-start.10
  65.4 6.2 %copy-start.9 = (f32[1,1024]{1,0:T(1,128)S(1)}, f32[1,1024]{1,0:T(1,128)}, u32[]{:S(2)}) copy-start(f32[1,1024]{1,0:T(1,128)} %param.9) | copy-start | bytes 12292
  66.0 70.1 %all-to-all-start.1 = ((f32[16,384,128]{1,2,0:T(8,128)}), f32[16,384,128]{1,2,0:T(8,128)S(1)}, u32[]{:S(2)}, u32[]{:S(2)}) async-start(f32[16,384,128]{1,2,0:T(8,128)} %bitcast.16), calls=%async_computation.2 | async-start | bytes 6291456 | tf_op jit(solution)/shard_map/all_to_all | solution.py:46
  70.7 70.0 %all-gather.13.cloned.1.call-start = ((), (), s32[]{:S(2)}) async-start(), calls=%async_computation.8 | async-start | bytes 3932160 | tf_op jit(solution)/shard_map/all_gather | solution.py:35
  74.2 126.3 %all-gather.11.cloned.1.call-start = ((), (), s32[]{:S(2)}) async-start(), calls=%async_computation.6 | async-start | bytes 1671168 | tf_op jit(solution)/shard_map/all_gather | solution.py:115
  136.9 127.6 %all-gather.17.cloned.1.call-start = ((), (), s32[]{:S(2)}) async-start(), calls=%async_computation.10 | async-start | bytes 3932160 | tf_op jit(solution)/shard_map/all_gather | solution.py:35
  140.6 60.0 %copy-start.8 = (bf16[384,128]{0,1:T(8,128)(2,1)S(1)}, bf16[384,128]{0,1:T(8,128)(2,1)}, u32[]{:S(2)}) copy-start(bf16[384,128]{0,1:T(8,128)(2,1)} %reduce_sum.81) | copy-start | bytes 294916
  140.7 192.8 %all-gather.15.cloned.1.call-start = ((), (), s32[]{:S(2)}) async-start(), calls=%async_computation.9 | async-start | bytes 3932160 | tf_op jit(solution)/shard_map/all_gather | solution.py:35
  144.4 235.0 %reduce-scatter.5.cloned.1.call-start = ((), (), s32[]{:S(2)}) async-start(), calls=%async_computation.7 | async-start | bytes 1179648 | tf_op jit(solution)/shard_map/reduce_scatter | solution.py:121
  203.6 63.4 %copy-start.7 = (bf16[1,384,1024]{2,1,0:T(8,128)(2,1)S(1)}, bf16[1,384,1024]{2,1,0:T(8,128)(2,1)}, u32[]{:S(2)}) copy-start(bf16[1,384,1024]{2,1,0:T(8,128)(2,1)} %param.7) | copy-start | bytes 2359300
  203.6 353.2 %reduce-scatter.3.cloned.1.call-start = ((), (), s32[]{:S(2)}) async-start(), calls=%async_computation.5 | async-start | bytes 9437184 | tf_op jit(solution)/shard_map/reduce_scatter | solution.py:52
  270.5 65.6 %copy-start.4 = (bf16[1,384,1024]{2,1,0:T(8,128)(2,1)S(1)}, bf16[1,384,1024]{2,1,0:T(8,128)(2,1)}, u32[]{:S(2)}) copy-start(bf16[1,384,1024]{2,1,0:T(8,128)(2,1)} %param.6) | copy-start | bytes 2359300
  270.5 65.6 %copy-start.6 = (bf16[384,1024]{1,0:T(8,128)(2,1)S(1)}, bf16[384,1024]{1,0:T(8,128)(2,1)}, u32[]{:S(2)}) copy-start(bf16[384,1024]{1,0:T(8,128)(2,1)} %copy-done.5) | copy-start | bytes 2359300
  336.1 2.2 copy-start.2
  342.5 216.6 %copy-start.1 = (bf16[1,52,52]{2,1,0:T(8,128)(2,1)S(1)}, bf16[1,52,52]{2,1,0:T(8,128)(2,1)}, u32[]{:S(2)}) copy-start(bf16[1,52,52]{2,1,0:T(8,128)(2,1)} %param.10) | copy-start | bytes 16228
Sparse Core Ops, SparseCore 0:
  11.4 45.8 all-gather.8
  74.4 62.6 all-gather.12
  140.1 60.3 all-gather.10
  202.2 62.1 all-gather.16
  266.1 67.3 all-gather.14
  335.9 43.5 reduce-scatter.4
  382.0 174.8 reduce-scatter.2
